TPU v7x, 256 devices: a whole 4x4x8 slice. The times are simulated.
256 devices in a mesh: snap: 4 (over y_hi, core), slab: 64 (over z, x, y_lo).
Axes of the slice: x: 4, y: 4 (y_hi: 2, y_lo: 2; y = y_hi * 2 + y_lo), z: 8, core: 2. Of those that a mesh axis runs over, the one named last changes fastest.
Arguments:
- velocity: bfloat16 [64, 3, 512, 16, 512], P('snap', None, 'slab'), may hold values from -6 to 6
- phase_bins: int32 [64], P('snap'), may hold values from 0 to 179, as said below
Outputs:
- coefficients: float32 [3, 3, 4, 512, 16, 512], P(None, None, None, 'slab', None, 'snap')
Inputs may be any that keep to these rules, and one draw needn't show every extreme that they name: `phase_bins`: no two snapshots share a bin, and the bins of all snapshots spread over the whole revolution.
All inputs are finite; a program needn't handle non-finite values.
Results may differ from a plain program's by a relative error of at most 0.0003.
Values may be sent and summed in bfloat16 or wider, within the bound.
A program may use at most 128 MiB of HBM per device.

v0:
```python
import jax
import jax.numpy as jnp
from jax import lax
from jax.sharding import PartitionSpec as P

BINS = 180


inv_spacing = 0.75


def extended(array, sides, width):
    for axis, dim in sides:
        peers, length = (lax.axis_size(axis), array.shape[dim])
        up = [(i, (i + 1) % peers) for i in range(peers - 1)]
        down = [(j, i) for i, j in up]
        last = lax.slice_in_dim(array, length - width, length, axis=dim)
        initial = lax.slice_in_dim(array, 0, width, axis=dim)
        before = lax.ppermute(last, axis, up)
        after = lax.ppermute(initial, axis, down)
        array = jnp.concatenate([before, array, after], axis=dim)
    return array


def central(padded, direction):
    extent = padded.shape[-3:]
    leading = [slice(None)] * (padded.ndim - 3)

    def shifted(offset):
        window = [slice(2, extent[0] - 2), slice(2, extent[1] - 2), slice(2, extent[2] - 2)]
        window[direction] = slice(offset, extent[direction] - 4 + offset)
        return padded[tuple(leading + window)].astype(jnp.float32)

    return (8.0 * (shifted(3) - shifted(1)) - (shifted(4) - shifted(0))) * (inv_spacing / 12.0)


def vorticity_of(comp_u, comp_v, comp_w):
    omega_x = central(comp_w, 1) - central(comp_v, 2)
    omega_y = central(comp_u, 2) - central(comp_w, 0)
    omega_z = central(comp_v, 0) - central(comp_u, 1)
    return jnp.stack([omega_x, omega_y, omega_z], axis=-4)


def basis_weights(phase_bins):
    centers = (jnp.arange(BINS, dtype=jnp.float32) + 0.5) * (2.0 * jnp.pi / BINS)
    table = jnp.stack([jnp.ones_like(centers), jnp.cos(centers), jnp.sin(centers)], axis=1)
    onehot = (phase_bins[:, None] == jnp.arange(BINS, dtype=jnp.int32)[None, :]).astype(jnp.float32)
    return jnp.dot(onehot, table, precision=lax.Precision.HIGHEST)


def invert_three(gram):
    g00, g01, g02 = (gram[0, 0], gram[0, 1], gram[0, 2])
    g10, g11, g12 = (gram[1, 0], gram[1, 1], gram[1, 2])
    g20, g21, g22 = (gram[2, 0], gram[2, 1], gram[2, 2])
    c00 = g11 * g22 - g12 * g21
    c01 = g02 * g21 - g01 * g22
    c02 = g01 * g12 - g02 * g11
    c10 = g12 * g20 - g10 * g22
    c11 = g00 * g22 - g02 * g20
    c12 = g02 * g10 - g00 * g12
    c20 = g10 * g21 - g11 * g20
    c21 = g01 * g20 - g00 * g21
    c22 = g00 * g11 - g01 * g10
    determinant = g00 * c00 + g01 * c10 + g02 * c20
    adjugate = jnp.stack(
        [jnp.stack([c00, c01, c02]), jnp.stack([c10, c11, c12]), jnp.stack([c20, c21, c22])]
    )
    return adjugate / determinant


def weighted_powers(weights, comp_u, comp_v, comp_w):

    def accumulate(total, inputs):
        weight_row, field_u, field_v, field_w = inputs
        omega = vorticity_of(field_u, field_v, field_w)
        squared = omega * omega
        powers = jnp.stack([omega, squared, squared * omega, squared * squared], axis=1)
        return (total + weight_row[:, None, None, None, None, None] * powers[None], None)

    shape_out = (
        weights.shape[1],
        3,
        4,
        comp_u.shape[1] - 4,
        comp_u.shape[2] - 4,
        comp_u.shape[3] - 4,
    )
    start = jnp.zeros(shape_out, jnp.float32)
    sums, _ = lax.scan(accumulate, start, (weights, comp_u, comp_v, comp_w))
    return sums


def local(velocity, phase_bins):
    all_bins = lax.all_gather(phase_bins, "snap", axis=0, tiled=True)
    all_weights = basis_weights(all_bins)
    gram = jnp.dot(all_weights.T, all_weights, precision=lax.Precision.HIGHEST)
    inverse = invert_three(gram)
    own_weights = basis_weights(phase_bins)
    side_planes = extended(velocity[:, 1:3], (("slab", 2),), 2)
    comp_u = jnp.pad(velocity[:, 0], ((0, 0), (2, 2), (2, 2), (2, 2)))
    comp_v = jnp.pad(side_planes[:, 0], ((0, 0), (0, 0), (2, 2), (2, 2)))
    comp_w = jnp.pad(side_planes[:, 1], ((0, 0), (0, 0), (2, 2), (2, 2)))
    partial_sums = weighted_powers(own_weights, comp_u, comp_v, comp_w)
    sums = lax.psum_scatter(partial_sums, "snap", scatter_dimension=5, tiled=True)
    return jnp.einsum("ij,j...->i...", inverse, sums, precision=lax.Precision.HIGHEST)


def solution(mesh):
    in_specs = (P("snap", None, "slab", None, None), P("snap"))
    out_specs = P(None, None, None, "slab", None, "snap")
    return jax.shard_map(local, mesh=mesh, in_specs=in_specs, out_specs=out_specs, check_vma=False)
```

profile of v0, /device:TPU:1, one launch (start us, length us, event | category | flops | bytes accessed | tf_op | source)
XLA Modules:
  0.0 456.7 jit_solution(5304131280495239679)
XLA Ops:
  9.4 5.0 %collective-permute-start = (bf16[16,2,2,16,512]{4,3,2,0,1:T(8,128)(2,1)}, bf16[16,2,2,16,512]{4,3,2,0,1:T(8,128)(2,1)}, u32[]{:S(2)}, u32[]{:S(2)}) collective-permute-start(bf16[16,2,2,16,512]{4,3,2,0,1:T(8,128)(2,1)} %copy.18), channel_id=1, source_target_pairs={{0,1},{1,2},{2,3},{3,4},{4,5},{5,6},{6,7},{7,8},{8,9},{9,10},{10,1... | collective-permute-start | bytes 3145736 | tf_op jit(solution)/shard_map/ppermute | solution.py:19
  15.9 3.3 slice_bitcast_fusion.2
  19.2 7.8 %pad.13 = bf16[16,12,20,516]{3,2,1,0:T(8,128)(2,1)} pad(bf16[16,8,16,512]{3,2,1,0:T(8,128)(2,1)} %slice_bitcast_fusion.2, bf16[]{:T(256)} %constant.26.clone.1), padding=0_0x2_2x2_2x2_2 | pad | bytes 6060034 | tf_op jit(solution)/shard_map/jit(_pad)/pad | solution.py:100
  27.2 30.9 %collective-permute-done = bf16[16,2,2,16,512]{4,3,2,0,1:T(8,128)(2,1)} collective-permute-done((bf16[16,2,2,16,512]{4,3,2,0,1:T(8,128)(2,1)}, bf16[16,2,2,16,512]{4,3,2,0,1:T(8,128)(2,1)}, u32[]{:S(2)}, u32[]{:S(2)}) %collective-permute-start) | collective-permute-done | bytes 1048608 | tf_op jit(solution)/shard_map/ppermute | solution.py:19
  63.0 7.3 %pad.12 = bf16[16,12,20,516]{3,2,1,0:T(8,128)(2,1)} pad(bf16[16,12,16,512]{3,2,1,0:T(8,128)(2,1)S(1)} %get-tuple-element.78, bf16[]{:T(256)} %constant.26.clone.1), padding=0_0x0_0x2_2x2_2 | pad | bytes 7108610 | tf_op jit(solution)/shard_map/jit(_pad)/pad | solution.py:101
  70.3 7.2 %pad.11 = bf16[16,12,20,516]{3,2,1,0:T(8,128)(2,1)} pad(bf16[16,12,16,512]{3,2,1,0:T(8,128)(2,1)S(1)} %get-tuple-element.79, bf16[]{:T(256)} %constant.26.clone.1), padding=0_0x0_0x2_2x2_2 | pad | bytes 7108610 | tf_op jit(solution)/shard_map/jit(_pad)/pad | solution.py:102
  77.5 267.3 %while.11 = (s32[]{:T(128)}, f32[3,3,4,8,16,512]{5,4,3,2,1,0:T(8,128)}, f32[16,3]{1,0:T(8,128)S(1)}, bf16[16,12,20,516]{3,2,1,0:T(8,128)(2,1)}, bf16[16,12,20,51...) while((s32[]{:T(128)}, ...), condition=%wide.region_1.2_spmd.clone, body=%wide.region_0.1_spmd.clone.sunk | while | flops 14548995 | bytes 113946064 | solution.py:89
  81.7 2.1 pad_maximum_fusion.6
  85.6 5.0 %select_add_fusion.2 = f32[3,3,4,8,16,512]{5,4,3,2,1,0:T(8,128)S(1)} fusion(f32[3,3,4,8,16,512]{5,4,3,2,1,0:T(8,128)S(1)} %copy-done, f32[3,4,8,16,512]{4,3,2,1,0:T(8,128)} %pad_maximum_fusion.6, f32[3]{0:T(128)S(1)} %fusion.29, pred[]{:T(512)S(6)} %compare.6), kind=kLoop, calls=%fused_computation.clone.1 | loop fusion | flops 7077888 | bytes 22020108 | tf_op jit(solution)/shard_map/while/body/eval_jaxpr/add | solution.py:78
  90.6 3.6 copy-done.1
  98.4 2.1 pad_maximum_fusion.6
  102.3 5.0 %select_add_fusion.2 = f32[3,3,4,8,16,512]{5,4,3,2,1,0:T(8,128)S(1)} fusion(f32[3,3,4,8,16,512]{5,4,3,2,1,0:T(8,128)S(1)} %copy-done, f32[3,4,8,16,512]{4,3,2,1,0:T(8,128)} %pad_maximum_fusion.6, f32[3]{0:T(128)S(1)} %fusion.29, pred[]{:T(512)S(6)} %compare.6), kind=kLoop, calls=%fused_computation.clone.1 | loop fusion | flops 7077888 | bytes 22020108 | tf_op jit(solution)/shard_map/while/body/eval_jaxpr/add | solution.py:78
  107.3 3.6 copy-done.1
  115.1 2.1 pad_maximum_fusion.6
  119.0 5.0 %select_add_fusion.2 = f32[3,3,4,8,16,512]{5,4,3,2,1,0:T(8,128)S(1)} fusion(f32[3,3,4,8,16,512]{5,4,3,2,1,0:T(8,128)S(1)} %copy-done, f32[3,4,8,16,512]{4,3,2,1,0:T(8,128)} %pad_maximum_fusion.6, f32[3]{0:T(128)S(1)} %fusion.29, pred[]{:T(512)S(6)} %compare.6), kind=kLoop, calls=%fused_computation.clone.1 | loop fusion | flops 7077888 | bytes 22020108 | tf_op jit(solution)/shard_map/while/body/eval_jaxpr/add | solution.py:78
  124.0 3.6 copy-done.1
  131.8 2.1 pad_maximum_fusion.6
  135.7 5.0 %select_add_fusion.2 = f32[3,3,4,8,16,512]{5,4,3,2,1,0:T(8,128)S(1)} fusion(f32[3,3,4,8,16,512]{5,4,3,2,1,0:T(8,128)S(1)} %copy-done, f32[3,4,8,16,512]{4,3,2,1,0:T(8,128)} %pad_maximum_fusion.6, f32[3]{0:T(128)S(1)} %fusion.29, pred[]{:T(512)S(6)} %compare.6), kind=kLoop, calls=%fused_computation.clone.1 | loop fusion | flops 7077888 | bytes 22020108 | tf_op jit(solution)/shard_map/while/body/eval_jaxpr/add | solution.py:78
  140.7 3.6 copy-done.1
  148.5 2.1 pad_maximum_fusion.6
  152.4 5.0 %select_add_fusion.2 = f32[3,3,4,8,16,512]{5,4,3,2,1,0:T(8,128)S(1)} fusion(f32[3,3,4,8,16,512]{5,4,3,2,1,0:T(8,128)S(1)} %copy-done, f32[3,4,8,16,512]{4,3,2,1,0:T(8,128)} %pad_maximum_fusion.6, f32[3]{0:T(128)S(1)} %fusion.29, pred[]{:T(512)S(6)} %compare.6), kind=kLoop, calls=%fused_computation.clone.1 | loop fusion | flops 7077888 | bytes 22020108 | tf_op jit(solution)/shard_map/while/body/eval_jaxpr/add | solution.py:78
  157.4 3.6 copy-done.1
  169.1 5.0 %select_add_fusion.2 = f32[3,3,4,8,16,512]{5,4,3,2,1,0:T(8,128)S(1)} fusion(f32[3,3,4,8,16,512]{5,4,3,2,1,0:T(8,128)S(1)} %copy-done, f32[3,4,8,16,512]{4,3,2,1,0:T(8,128)} %pad_maximum_fusion.6, f32[3]{0:T(128)S(1)} %fusion.29, pred[]{:T(512)S(6)} %compare.6), kind=kLoop, calls=%fused_computation.clone.1 | loop fusion | flops 7077888 | bytes 22020108 | tf_op jit(solution)/shard_map/while/body/eval_jaxpr/add | solution.py:78
  174.1 3.6 copy-done.1
  185.8 5.0 %select_add_fusion.2 = f32[3,3,4,8,16,512]{5,4,3,2,1,0:T(8,128)S(1)} fusion(f32[3,3,4,8,16,512]{5,4,3,2,1,0:T(8,128)S(1)} %copy-done, f32[3,4,8,16,512]{4,3,2,1,0:T(8,128)} %pad_maximum_fusion.6, f32[3]{0:T(128)S(1)} %fusion.29, pred[]{:T(512)S(6)} %compare.6), kind=kLoop, calls=%fused_computation.clone.1 | loop fusion | flops 7077888 | bytes 22020108 | tf_op jit(solution)/shard_map/while/body/eval_jaxpr/add | solution.py:78
  190.8 3.6 copy-done.1
  202.5 5.0 %select_add_fusion.2 = f32[3,3,4,8,16,512]{5,4,3,2,1,0:T(8,128)S(1)} fusion(f32[3,3,4,8,16,512]{5,4,3,2,1,0:T(8,128)S(1)} %copy-done, f32[3,4,8,16,512]{4,3,2,1,0:T(8,128)} %pad_maximum_fusion.6, f32[3]{0:T(128)S(1)} %fusion.29, pred[]{:T(512)S(6)} %compare.6), kind=kLoop, calls=%fused_computation.clone.1 | loop fusion | flops 7077888 | bytes 22020108 | tf_op jit(solution)/shard_map/while/body/eval_jaxpr/add | solution.py:78
  207.5 3.6 copy-done.1
  219.2 5.0 %select_add_fusion.2 = f32[3,3,4,8,16,512]{5,4,3,2,1,0:T(8,128)S(1)} fusion(f32[3,3,4,8,16,512]{5,4,3,2,1,0:T(8,128)S(1)} %copy-done, f32[3,4,8,16,512]{4,3,2,1,0:T(8,128)} %pad_maximum_fusion.6, f32[3]{0:T(128)S(1)} %fusion.29, pred[]{:T(512)S(6)} %compare.6), kind=kLoop, calls=%fused_computation.clone.1 | loop fusion | flops 7077888 | bytes 22020108 | tf_op jit(solution)/shard_map/while/body/eval_jaxpr/add | solution.py:78
  224.2 3.6 copy-done.1
  235.9 5.0 %select_add_fusion.2 = f32[3,3,4,8,16,512]{5,4,3,2,1,0:T(8,128)S(1)} fusion(f32[3,3,4,8,16,512]{5,4,3,2,1,0:T(8,128)S(1)} %copy-done, f32[3,4,8,16,512]{4,3,2,1,0:T(8,128)} %pad_maximum_fusion.6, f32[3]{0:T(128)S(1)} %fusion.29, pred[]{:T(512)S(6)} %compare.6), kind=kLoop, calls=%fused_computation.clone.1 | loop fusion | flops 7077888 | bytes 22020108 | tf_op jit(solution)/shard_map/while/body/eval_jaxpr/add | solution.py:78
  240.9 3.6 copy-done.1
  248.8 2.1 pad_maximum_fusion.6
  252.6 5.0 %select_add_fusion.2 = f32[3,3,4,8,16,512]{5,4,3,2,1,0:T(8,128)S(1)} fusion(f32[3,3,4,8,16,512]{5,4,3,2,1,0:T(8,128)S(1)} %copy-done, f32[3,4,8,16,512]{4,3,2,1,0:T(8,128)} %pad_maximum_fusion.6, f32[3]{0:T(128)S(1)} %fusion.29, pred[]{:T(512)S(6)} %compare.6), kind=kLoop, calls=%fused_computation.clone.1 | loop fusion | flops 7077888 | bytes 22020108 | tf_op jit(solution)/shard_map/while/body/eval_jaxpr/add | solution.py:78
  257.6 3.6 copy-done.1
  269.3 5.0 %select_add_fusion.2 = f32[3,3,4,8,16,512]{5,4,3,2,1,0:T(8,128)S(1)} fusion(f32[3,3,4,8,16,512]{5,4,3,2,1,0:T(8,128)S(1)} %copy-done, f32[3,4,8,16,512]{4,3,2,1,0:T(8,128)} %pad_maximum_fusion.6, f32[3]{0:T(128)S(1)} %fusion.29, pred[]{:T(512)S(6)} %compare.6), kind=kLoop, calls=%fused_computation.clone.1 | loop fusion | flops 7077888 | bytes 22020108 | tf_op jit(solution)/shard_map/while/body/eval_jaxpr/add | solution.py:78
  274.3 3.6 copy-done.1
  286.0 5.0 %select_add_fusion.2 = f32[3,3,4,8,16,512]{5,4,3,2,1,0:T(8,128)S(1)} fusion(f32[3,3,4,8,16,512]{5,4,3,2,1,0:T(8,128)S(1)} %copy-done, f32[3,4,8,16,512]{4,3,2,1,0:T(8,128)} %pad_maximum_fusion.6, f32[3]{0:T(128)S(1)} %fusion.29, pred[]{:T(512)S(6)} %compare.6), kind=kLoop, calls=%fused_computation.clone.1 | loop fusion | flops 7077888 | bytes 22020108 | tf_op jit(solution)/shard_map/while/body/eval_jaxpr/add | solution.py:78
  291.0 3.6 copy-done.1
  302.8 5.0 %select_add_fusion.2 = f32[3,3,4,8,16,512]{5,4,3,2,1,0:T(8,128)S(1)} fusion(f32[3,3,4,8,16,512]{5,4,3,2,1,0:T(8,128)S(1)} %copy-done, f32[3,4,8,16,512]{4,3,2,1,0:T(8,128)} %pad_maximum_fusion.6, f32[3]{0:T(128)S(1)} %fusion.29, pred[]{:T(512)S(6)} %compare.6), kind=kLoop, calls=%fused_computation.clone.1 | loop fusion | flops 7077888 | bytes 22020108 | tf_op jit(solution)/shard_map/while/body/eval_jaxpr/add | solution.py:78
  307.8 3.6 copy-done.1
  319.5 5.0 %select_add_fusion.2 = f32[3,3,4,8,16,512]{5,4,3,2,1,0:T(8,128)S(1)} fusion(f32[3,3,4,8,16,512]{5,4,3,2,1,0:T(8,128)S(1)} %copy-done, f32[3,4,8,16,512]{4,3,2,1,0:T(8,128)} %pad_maximum_fusion.6, f32[3]{0:T(128)S(1)} %fusion.29, pred[]{:T(512)S(6)} %compare.6), kind=kLoop, calls=%fused_computation.clone.1 | loop fusion | flops 7077888 | bytes 22020108 | tf_op jit(solution)/shard_map/while/body/eval_jaxpr/add | solution.py:78
  324.5 3.6 copy-done.1
  336.2 5.0 %select_add_fusion.2 = f32[3,3,4,8,16,512]{5,4,3,2,1,0:T(8,128)S(1)} fusion(f32[3,3,4,8,16,512]{5,4,3,2,1,0:T(8,128)S(1)} %copy-done, f32[3,4,8,16,512]{4,3,2,1,0:T(8,128)} %pad_maximum_fusion.6, f32[3]{0:T(128)S(1)} %fusion.29, pred[]{:T(512)S(6)} %compare.6), kind=kLoop, calls=%fused_computation.clone.1 | loop fusion | flops 7077888 | bytes 22020108 | tf_op jit(solution)/shard_map/while/body/eval_jaxpr/add | solution.py:78
  341.2 3.6 copy-done.1
  347.0 6.5 %all-reduce.3 = s32[64]{0:T(128)S(1)} all-reduce(s32[64]{0:T(128)S(1)} %dynamic-update-slice), channel_id=1, replica_groups=mesh['snap'=4,'slab'=64] {'snap'}, use_global_device_ids=true, to_apply=%add.3 | all-reduce | flops 64 | bytes 512
  379.9 59.4 %reduce-scatter.2.cloned.1.call-done = f32[3,3,4,8,16,128]{5,4,3,2,1,0:T(8,128)} async-done(((f32[3,3,4,8,16,512]{5,4,3,2,1,0:T(8,128)}), f32[3,3,4,8,16,128]{5,4,3,2,1,0:T(8,128)}) %reduce-scatter.2.cloned.1.call-update) | async-done | bytes 2359312 | tf_op jit(solution)/shard_map/reduce_scatter | solution.py:104
  439.2 8.8 %fusion.4 = f32[3,3,4,8,16,128]{5,0,4,3,2,1:T(4,128)S(1)} fusion(f32[3,3,4,8,16,128]{5,4,3,2,1,0:T(8,128)} %reduce-scatter.2.cloned.1.call-done, f32[1,3]{1,0:T(1,128)S(1)} %maximum_bitcast_fusion.3, f32[1,3]{1,0:T(1,128)S(1)} %maximum_bitcast_fusion.2, f32[1,3]{1,0:T(1,128)S(1)} %maximum_bitcast_fusion.1, f32[]{:T(128)S(6)} %add.39), kind=kOutput, calls=%fused_computation.18 | convolution fusion | flops 21233692 | bytes 4718632 | tf_op jit(solution)/shard_map/ij,j...->i.../dot_general | solution.py:105
  (204 shorter events, 129.9 us)
Async XLA Ops:
  6.5 432.7 %reduce-scatter.2.cloned.1.call-start = ((), (), s32[]{:S(2)}) async-start(), calls=%async_computation.1 | async-start | bytes 11796480 | tf_op jit(solution)/shard_map/reduce_scatter | solution.py:104
  9.4 48.6 %collective-permute-start = (bf16[16,2,2,16,512]{4,3,2,0,1:T(8,128)(2,1)}, bf16[16,2,2,16,512]{4,3,2,0,1:T(8,128)(2,1)}, u32[]{:S(2)}, u32[]{:S(2)}) collective-permute-start(bf16[16,2,2,16,512]{4,3,2,0,1:T(8,128)(2,1)} %copy.18), channel_id=1, source_target_pairs={{0,1},{1,2},{2,3},{3,4},{4,5},{5,6},{6,7},{7,8},{8,9},{9,10},{10,1... | collective-permute-start | bytes 3145736 | tf_op jit(solution)/shard_map/ppermute | solution.py:19
  14.5 12.5 %copy-start.2 = (s32[16]{0:T(128)S(1)}, s32[16]{0:T(128)}, u32[]{:S(2)}) copy-start(s32[16]{0:T(128)} %param.5) | copy-start | bytes 196
  14.5 45.9 %collective-permute-start.1 = (bf16[16,2,2,16,512]{4,3,2,0,1:T(8,128)(2,1)S(1)}, bf16[16,2,2,16,512]{4,3,2,0,1:T(8,128)(2,1)}, u32[]{:S(2)}, u32[]{:S(2)}) collective-permute-start(bf16[16,2,2,16,512]{4,3,2,0,1:T(8,128)(2,1)S(1)} %copy.20), channel_id=1, source_target_pairs={{1,0},{2,1},{3,2},{4,3},{5,4},{6,5},{7,6},{8,7},{9,8},{10,9},{11,1... | collective-permute-start | bytes 3145736 | tf_op jit(solution)/shard_map/ppermute | solution.py:20
  15.8 43.5 %slice-start = ((s8[6291456]{0:T(1024)(128)(4,1)}), s8[2097152]{0:T(1024)(128)(4,1)S(1)}, s32[]{:S(2)}) async-start(s8[6291456]{0:T(1024)(128)(4,1)} %bitcast.85), calls=%async_computation.2 | async-start | bytes 4194304
  19.2 40.2 %slice-start.1 = ((s8[6291456]{0:T(1024)(128)(4,1)}), s8[4194304]{0:T(1024)(128)(4,1)S(1)}, s32[]{:S(2)}) async-start(s8[6291456]{0:T(1024)(128)(4,1)} %bitcast.85), calls=%async_computation.3 | async-start | bytes 8388608
  80.8 4.8 %copy-start = (f32[3,3,4,8,16,512]{5,4,3,2,1,0:T(8,128)S(1)}, f32[3,3,4,8,16,512]{5,4,3,2,1,0:T(8,128)}, u32[]{:S(2)}) copy-start(f32[3,3,4,8,16,512]{5,4,3,2,1,0:T(8,128)} %get-tuple-element.153) | copy-start | bytes 28311556 | tf_op jit(solution)/shard_map/while
  90.6 3.7 copy-start.1
  97.5 4.8 %copy-start = (f32[3,3,4,8,16,512]{5,4,3,2,1,0:T(8,128)S(1)}, f32[3,3,4,8,16,512]{5,4,3,2,1,0:T(8,128)}, u32[]{:S(2)}) copy-start(f32[3,3,4,8,16,512]{5,4,3,2,1,0:T(8,128)} %get-tuple-element.153) | copy-start | bytes 28311556 | tf_op jit(solution)/shard_map/while
  107.3 3.7 copy-start.1
  114.2 4.8 %copy-start = (f32[3,3,4,8,16,512]{5,4,3,2,1,0:T(8,128)S(1)}, f32[3,3,4,8,16,512]{5,4,3,2,1,0:T(8,128)}, u32[]{:S(2)}) copy-start(f32[3,3,4,8,16,512]{5,4,3,2,1,0:T(8,128)} %get-tuple-element.153) | copy-start | bytes 28311556 | tf_op jit(solution)/shard_map/while
  124.0 3.7 copy-start.1
  130.9 4.8 %copy-start = (f32[3,3,4,8,16,512]{5,4,3,2,1,0:T(8,128)S(1)}, f32[3,3,4,8,16,512]{5,4,3,2,1,0:T(8,128)}, u32[]{:S(2)}) copy-start(f32[3,3,4,8,16,512]{5,4,3,2,1,0:T(8,128)} %get-tuple-element.153) | copy-start | bytes 28311556 | tf_op jit(solution)/shard_map/while
  140.7 3.7 copy-start.1
  147.6 4.8 %copy-start = (f32[3,3,4,8,16,512]{5,4,3,2,1,0:T(8,128)S(1)}, f32[3,3,4,8,16,512]{5,4,3,2,1,0:T(8,128)}, u32[]{:S(2)}) copy-start(f32[3,3,4,8,16,512]{5,4,3,2,1,0:T(8,128)} %get-tuple-element.153) | copy-start | bytes 28311556 | tf_op jit(solution)/shard_map/while
  157.4 3.7 copy-start.1
  164.3 4.8 %copy-start = (f32[3,3,4,8,16,512]{5,4,3,2,1,0:T(8,128)S(1)}, f32[3,3,4,8,16,512]{5,4,3,2,1,0:T(8,128)}, u32[]{:S(2)}) copy-start(f32[3,3,4,8,16,512]{5,4,3,2,1,0:T(8,128)} %get-tuple-element.153) | copy-start | bytes 28311556 | tf_op jit(solution)/shard_map/while
  174.1 3.7 copy-start.1
  181.0 4.8 %copy-start = (f32[3,3,4,8,16,512]{5,4,3,2,1,0:T(8,128)S(1)}, f32[3,3,4,8,16,512]{5,4,3,2,1,0:T(8,128)}, u32[]{:S(2)}) copy-start(f32[3,3,4,8,16,512]{5,4,3,2,1,0:T(8,128)} %get-tuple-element.153) | copy-start | bytes 28311556 | tf_op jit(solution)/shard_map/while
  190.8 3.7 copy-start.1
  197.7 4.8 %copy-start = (f32[3,3,4,8,16,512]{5,4,3,2,1,0:T(8,128)S(1)}, f32[3,3,4,8,16,512]{5,4,3,2,1,0:T(8,128)}, u32[]{:S(2)}) copy-start(f32[3,3,4,8,16,512]{5,4,3,2,1,0:T(8,128)} %get-tuple-element.153) | copy-start | bytes 28311556 | tf_op jit(solution)/shard_map/while
  207.5 3.7 copy-start.1
  214.4 4.8 %copy-start = (f32[3,3,4,8,16,512]{5,4,3,2,1,0:T(8,128)S(1)}, f32[3,3,4,8,16,512]{5,4,3,2,1,0:T(8,128)}, u32[]{:S(2)}) copy-start(f32[3,3,4,8,16,512]{5,4,3,2,1,0:T(8,128)} %get-tuple-element.153) | copy-start | bytes 28311556 | tf_op jit(solution)/shard_map/while
  224.2 3.7 copy-start.1
  231.1 4.8 %copy-start = (f32[3,3,4,8,16,512]{5,4,3,2,1,0:T(8,128)S(1)}, f32[3,3,4,8,16,512]{5,4,3,2,1,0:T(8,128)}, u32[]{:S(2)}) copy-start(f32[3,3,4,8,16,512]{5,4,3,2,1,0:T(8,128)} %get-tuple-element.153) | copy-start | bytes 28311556 | tf_op jit(solution)/shard_map/while
  240.9 3.7 copy-start.1
  247.8 4.8 %copy-start = (f32[3,3,4,8,16,512]{5,4,3,2,1,0:T(8,128)S(1)}, f32[3,3,4,8,16,512]{5,4,3,2,1,0:T(8,128)}, u32[]{:S(2)}) copy-start(f32[3,3,4,8,16,512]{5,4,3,2,1,0:T(8,128)} %get-tuple-element.153) | copy-start | bytes 28311556 | tf_op jit(solution)/shard_map/while
  257.6 3.7 copy-start.1
  264.5 4.8 %copy-start = (f32[3,3,4,8,16,512]{5,4,3,2,1,0:T(8,128)S(1)}, f32[3,3,4,8,16,512]{5,4,3,2,1,0:T(8,128)}, u32[]{:S(2)}) copy-start(f32[3,3,4,8,16,512]{5,4,3,2,1,0:T(8,128)} %get-tuple-element.153) | copy-start | bytes 28311556 | tf_op jit(solution)/shard_map/while
  274.3 3.7 copy-start.1
  281.2 4.8 %copy-start = (f32[3,3,4,8,16,512]{5,4,3,2,1,0:T(8,128)S(1)}, f32[3,3,4,8,16,512]{5,4,3,2,1,0:T(8,128)}, u32[]{:S(2)}) copy-start(f32[3,3,4,8,16,512]{5,4,3,2,1,0:T(8,128)} %get-tuple-element.153) | copy-start | bytes 28311556 | tf_op jit(solution)/shard_map/while
  291.0 3.7 copy-start.1
  297.9 4.8 %copy-start = (f32[3,3,4,8,16,512]{5,4,3,2,1,0:T(8,128)S(1)}, f32[3,3,4,8,16,512]{5,4,3,2,1,0:T(8,128)}, u32[]{:S(2)}) copy-start(f32[3,3,4,8,16,512]{5,4,3,2,1,0:T(8,128)} %get-tuple-element.153) | copy-start | bytes 28311556 | tf_op jit(solution)/shard_map/while
  307.7 3.7 copy-start.1
  314.6 4.8 %copy-start = (f32[3,3,4,8,16,512]{5,4,3,2,1,0:T(8,128)S(1)}, f32[3,3,4,8,16,512]{5,4,3,2,1,0:T(8,128)}, u32[]{:S(2)}) copy-start(f32[3,3,4,8,16,512]{5,4,3,2,1,0:T(8,128)} %get-tuple-element.153) | copy-start | bytes 28311556 | tf_op jit(solution)/shard_map/while
  324.5 3.7 copy-start.1
  331.4 4.8 %copy-start = (f32[3,3,4,8,16,512]{5,4,3,2,1,0:T(8,128)S(1)}, f32[3,3,4,8,16,512]{5,4,3,2,1,0:T(8,128)}, u32[]{:S(2)}) copy-start(f32[3,3,4,8,16,512]{5,4,3,2,1,0:T(8,128)} %get-tuple-element.153) | copy-start | bytes 28311556 | tf_op jit(solution)/shard_map/while
  341.2 3.7 copy-start.1
  344.8 0.7 copy-start.3
Sparse Core Ops, SparseCore 0:
  345.0 94.2 reduce-scatter.1
where the time goes:
time: 459 us; the launch traced here: 457 us
  local copies, waits for them, and re-layouts  159 us (35%)
  other arithmetic  145 us (32%)
  waiting for transfers between devices  90.2 us (20%)
  between operations  39.2 us (9%)
  matrix products  9.46 us (2%)
  blocking collectives  6.49 us (1%)
  starting transfers between devices  6.29 us (1%)
    while x64, local copies, waits for them, and re-layouts  87 us
    add x16, other arithmetic, accumulate(): total + weight_row[:, None, None, None, None, None] * powers[None]  79.7 us
    reduce_scatter x1, waiting for transfers between devices, local(): lax.psum_scatter(partial_sums, 'snap', scatter_dimension=5, tiled=True)  59.4 us
    squeeze x32, local copies, waits for them, and re-layouts, weighted_powers(): sums, _ = lax.scan(accumulate, start, (weights, comp_u, comp_v, comp_w))  35 us
    another operation x32, other arithmetic, accumulate(): jnp.stack([omega, squared, squared * omega, squared * squared], axis=1)  34.2 us
    ppermute x1, waiting for transfers between devices, extended(): before = lax.ppermute(last, axis, up)  30.9 us
    sub x16, other arithmetic, vorticity_of(): omega_x = central(comp_w, 1) - central(comp_v, 2)  16.7 us
    sub x16, other arithmetic, vorticity_of(): omega_z = central(comp_v, 0) - central(comp_u, 1)  9.35 us
  transfers between devices with their start and end apart: 3, of which 2 were waited for; matrix products, arithmetic and copies ran while one was open for 3% of the time, Pallas kernels for 0%

commit v1 on v0

v1 whole, which is shorter than its diff:
```python
import functools

import jax
import jax.numpy as jnp
import numpy as np
from jax import lax
from jax.experimental import pallas as pl
from jax.experimental.pallas import tpu as pltpu
from jax.sharding import PartitionSpec as P

MESH = pl.DeviceIdType.MESH
BINS = 180
NEAR = 0.75 * 8.0 / 12.0
WIDE = 0.75 / 12.0
PLANES = ((2, 3, 4, 5), (0, 1, 6, 7))
NS, NP, NY, NZ = 16, 8, 16, 512
LANES = 128


def band(n):
    d = np.zeros((n, n), np.float32)
    for i in range(n):
        for o, c in ((1, NEAR), (-1, -NEAR), (2, -WIDE), (-2, WIDE)):
            if 0 <= i + o < n:
                d[i, i + o] = c
    return d


def stencils():
    along_y = np.kron(np.eye(NP, dtype=np.float32), band(NY))
    along_x = np.kron(band(NP + 4), np.eye(NY, dtype=np.float32))
    left_w, left_vu, left_halo = [], [], []
    for planes in PLANES:
        rows = np.concatenate([np.arange(p * NY, (p + 1) * NY) for p in planes])
        dy = along_y[rows]
        dx_ext = along_x[rows + 2 * NY]
        dx = dx_ext[:, 2 * NY : 2 * NY + NP * NY]
        halo = np.concatenate([dx_ext[:, : 2 * NY], dx_ext[:, -2 * NY :]], axis=1)
        left_w.append(np.concatenate([dy, -dx], axis=0))
        left_vu.append(np.concatenate([dx, -dy], axis=1))
        left_halo.append(halo)
    return [
        np.stack(left_w),
        np.stack(left_vu),
        left_halo[1],
        band(NZ).T.copy(),
    ]


def dot(a, b):
    return jnp.dot(a, b, preferred_element_type=jnp.float32)


def kernel(
    vel_hbm, bins, left_w, left_vu, left_halo, right_z, out,
    vel, halo, omega, weights, sums, mate, cross_out, cross_in, gram_out, gram_in,
    load_sem, halo_send, halo_recv, mate_send, mate_recv, cross_send, cross_recv, gram_send, gram_recv,
):
    snap, slab = lax.axis_index("snap"), lax.axis_index("slab")
    slabs = lax.axis_size("slab")
    core, chip = snap % 2, snap // 2
    has_lo, has_hi = slab > 0, slab < slabs - 1
    lo_peer = (snap, jnp.maximum(slab - 1, 0))
    hi_peer = (snap, jnp.minimum(slab + 1, slabs - 1))
    mate_peer = (chip * 2 + 1 - core, slab)
    cross_peer = ((1 - chip) * 2 + core, slab)
    snap_peers = [((snap + d) % 4, slab) for d in (1, 2, 3)]

    def zone(i):
        side = (chip + 1 - i // 2) % 2
        return pl.ds(pl.multiple_of((side * 2 + (core + 1 + i) % 2) * LANES, LANES), LANES)

    load = pltpu.make_async_copy(vel_hbm, vel, load_sem)
    load.start()

    barrier = pltpu.get_barrier_semaphore()
    for peer in snap_peers:
        pl.semaphore_signal(barrier, inc=1, device_id=peer, device_id_type=MESH)
    for cond, peer in ((has_lo, lo_peer), (has_hi, hi_peer)):
        @pl.when(cond)
        def _(peer=peer):
            pl.semaphore_signal(barrier, inc=1, device_id=peer, device_id_type=MESH)
    pl.semaphore_wait(barrier, 3 + has_lo.astype(jnp.int32) + has_hi.astype(jnp.int32))

    def halo_copy(i, side):
        planes = pl.ds(NP - 2, 2) if side == 0 else pl.ds(0, 2)
        return pltpu.make_async_remote_copy(
            src_ref=vel_hbm.at[:, pl.ds(1, 2), planes, :, zone(i)],
            dst_ref=halo.at[i, :, :, side],
            send_sem=halo_send.at[i, side],
            recv_sem=halo_recv.at[i, side],
            device_id=hi_peer if side == 0 else lo_peer,
            device_id_type=MESH,
        )

    for i in range(4):
        for side, cond in ((0, has_hi), (1, has_lo)):
            @pl.when(cond)
            def _(i=i, side=side):
                halo_copy(i, side).start()

    for side, cond in ((0, has_lo), (1, has_hi)):
        @pl.when(jnp.logical_not(cond))
        def _(side=side):
            for i in range(4):
                halo[i, :, :, side] = jnp.zeros((NS, 2, 2, NY, LANES), jnp.bfloat16)

    zero = jnp.zeros((8, LANES), jnp.float32)

    def weigh(s, g):
        angle = (jnp.full((8, LANES), bins[s], jnp.int32).astype(jnp.float32) + 0.5) * (
            2.0 * np.pi / BINS
        )
        c, n = jnp.cos(angle), jnp.sin(angle)
        weights[0, s] = c
        weights[1, s] = n
        return (g[0] + c, g[1] + n, g[2] + c * c, g[3] + c * n, g[4] + n * n)

    for n, value in enumerate(lax.fori_loop(0, NS, weigh, (zero,) * 5)):
        gram_out[n] = value

    def gram_copy(d):
        return pltpu.make_async_remote_copy(
            src_ref=gram_out, dst_ref=gram_in.at[d],
            send_sem=gram_send.at[d], recv_sem=gram_recv.at[d],
            device_id=snap_peers[d], device_id_type=MESH,
        )

    load.wait()

    def derive(i, p):
        z = zone(i)
        planes = PLANES[p]

        def own(s, comp):
            if p == 0:
                return vel[s, comp, 2:6].reshape(64, NZ)
            return jnp.concatenate([vel[s, comp, 0:2], vel[s, comp, 6:8]], axis=0).reshape(64, NZ)

        def body(s, carry):
            uv = jnp.concatenate([own(s, 0), own(s, 1)], axis=0)
            dz = dot(uv, right_z[:, z])
            v_u = jnp.concatenate(
                [vel[s, 1, :, :, z].reshape(NP * NY, LANES), vel[s, 0, :, :, z].reshape(NP * NY, LANES)],
                axis=0,
            )
            w = vel[s, 2, :, :, z].reshape(NP * NY, LANES)
            from_w = dot(left_w[p], w)
            om_z = dot(left_vu[p], v_u)
            om_x = from_w[:64] - dz[64:]
            om_y = from_w[64:] + dz[:64]
            if p == 1:
                v_halo = halo[i, s, 0].reshape(64, LANES)
                w_halo = halo[i, s, 1].reshape(64, LANES)
                om_z = om_z + dot(left_halo[...], v_halo)
                om_y = om_y - dot(left_halo[...], w_halo)
            omega[s, 0] = om_x.reshape(8, 8, LANES)
            omega[s, 1] = om_y.reshape(8, 8, LANES)
            omega[s, 2] = om_z.reshape(8, 8, LANES)
            return carry

        lax.fori_loop(0, NS, body, 0)

    def accumulate(i, p):
        def body(t, carry):
            c, r = t // 4, t % 4
            rows = pl.ds(2 * r, 2)
            acc = [[None] * 4 for _ in range(3)]
            for s in range(NS):
                om = omega[s, c, rows]
                sq = om * om
                powers = (om, sq, sq * om, sq * sq)
                for k in range(4):
                    for j in range(3):
                        term = powers[k] if j == 0 else weights[j - 1, s][None] * powers[k]
                        acc[j][k] = term if s == 0 else acc[j][k] + term
            for j in range(3):
                for k in range(4):
                    sums[i, p, j, c * 4 + k, rows] = acc[j][k]
            return carry

        lax.fori_loop(0, 12, body, 0)

    def mate_copy(half, p):
        return pltpu.make_async_remote_copy(
            src_ref=sums.at[2 * half, p], dst_ref=mate.at[half, p],
            send_sem=mate_send.at[half, p], recv_sem=mate_recv.at[half, p],
            device_id=mate_peer, device_id_type=MESH,
        )

    def cross_copy(p):
        return pltpu.make_async_remote_copy(
            src_ref=cross_out.at[p], dst_ref=cross_in.at[p],
            send_sem=cross_send.at[p], recv_sem=cross_recv.at[p],
            device_id=cross_peer, device_id_type=MESH,
        )

    for p in range(2):
        for i in range(4):
            if p == 1:
                for side, cond, gone in ((0, has_lo, has_hi), (1, has_hi, has_lo)):
                    @pl.when(cond)
                    def _(i=i, side=side):
                        halo_copy(i, side).wait_recv()
            derive(i, p)
            accumulate(i, p)
            if p == 0 and i == 0:
                for d in range(3):
                    gram_copy(d).start()
            if i % 2 == 0:
                mate_copy(i // 2, p).start()
            if i == 1:
                mate_copy(0, p).wait_recv()

                def add(t, carry, p=p):
                    for j in range(3):
                        cross_out[p, j, t] = sums[1, p, j, t] + mate[0, p, j, t]
                    return carry

                lax.fori_loop(0, 12, add, 0)
                cross_copy(p).start()

    for d in range(3):
        gram_copy(d).wait()
    g = [gram_out[n] + gram_in[0, n] + gram_in[1, n] + gram_in[2, n] for n in range(5)]
    g00 = jnp.full((8, LANES), 4.0 * NS, jnp.float32)
    g01, g02, g11, g12, g22 = g
    c00 = g11 * g22 - g12 * g12
    c01 = g02 * g12 - g01 * g22
    c02 = g01 * g12 - g02 * g11
    c11 = g00 * g22 - g02 * g02
    c12 = g02 * g01 - g00 * g12
    c22 = g00 * g11 - g01 * g01
    det = g00 * c00 + g01 * c01 + g02 * c02
    inverse = [[x / det for x in row] for row in ((c00, c01, c02), (c01, c11, c12), (c02, c12, c22))]

    for p in range(2):
        mate_copy(1, p).wait_recv()
        cross_copy(p).wait_recv()

        def solve(t, carry, p=p):
            total = [sums[3, p, j, t] + mate[1, p, j, t] + cross_in[p, j, t] for j in range(3)]
            for n in range(3):
                fit = sum(inverse[n][j][None] * total[j] for j in range(3)).reshape(4, NY, LANES)
                if p == 0:
                    out[n, t // 4, t % 4, 2:6] = fit
                else:
                    out[n, t // 4, t % 4, 0:2] = fit[:2]
                    out[n, t // 4, t % 4, 6:8] = fit[2:]
            return carry

        lax.fori_loop(0, 12, solve, 0)

    for i in range(4):
        for side, cond in ((0, has_hi), (1, has_lo)):
            @pl.when(cond)
            def _(i=i, side=side):
                halo_copy(i, side).wait_send()
    for p in range(2):
        cross_copy(p).wait_send()
        for half in range(2):
            mate_copy(half, p).wait_send()


def local(velocity, phase_bins):
    consts = [jnp.asarray(m, jnp.bfloat16) for m in stencils()]
    vmem = pl.BlockSpec(memory_space=pltpu.VMEM)
    f32, bf16, dma = jnp.float32, jnp.bfloat16, pltpu.SemaphoreType.DMA
    block = (3, 12, 8, 8, LANES)
    return pl.pallas_call(
        kernel,
        out_shape=jax.ShapeDtypeStruct((3, 3, 4, NP, NY, LANES), f32),
        in_specs=[pl.BlockSpec(memory_space=pl.ANY), pl.BlockSpec(memory_space=pltpu.SMEM)] + [vmem] * 4,
        out_specs=vmem,
        scratch_shapes=[
            pltpu.VMEM((NS, 3, NP, NY, NZ), bf16),
            pltpu.VMEM((4, NS, 2, 2, 2, NY, LANES), bf16),
            pltpu.VMEM((NS, 3, 8, 8, LANES), f32),
            pltpu.VMEM((2, NS, 8, LANES), f32),
            pltpu.VMEM((4, 2) + block, f32),
            pltpu.VMEM((2, 2) + block, f32),
            pltpu.VMEM((2,) + block, f32),
            pltpu.VMEM((2,) + block, f32),
            pltpu.VMEM((5, 8, LANES), f32),
            pltpu.VMEM((3, 5, 8, LANES), f32),
            dma, dma((4, 2)), dma((4, 2)), dma((2, 2)), dma((2, 2)), dma((2,)), dma((2,)), dma((3,)), dma((3,)),
        ],
        compiler_params=pltpu.CompilerParams(collective_id=0, has_side_effects=True),
    )(velocity, phase_bins, *consts)


def solution(mesh):
    in_specs = (P("snap", None, "slab", None, None), P("snap"))
    out_specs = P(None, None, None, "slab", None, "snap")
    return jax.shard_map(local, mesh=mesh, in_specs=in_specs, out_specs=out_specs, check_vma=False)
```

time: 459 us -> 110 us (0.24)
  local copies, waits for them, and re-layouts: 159 us -> 3.32 us
  other arithmetic: 145 us -> 0 us
  Pallas kernels: 0 us -> 107 us
  waiting for transfers between devices: 90.2 us -> 0 us
  between operations: 39.2 us -> 0.01 us
  matrix products: 9.46 us -> 0 us
  blocking collectives: 6.49 us -> 0 us
  starting transfers between devices: 6.29 us -> 0 us
    pallas_call x0 -> x1, Pallas kernels: none -> 107 us  [local(): pl.pallas_call(kernel, out_shape=jax.ShapeDtypeStruct((3, 3, 4, NP, NY, L...]
    while x64 -> x0, local copies, waits for them, and re-layouts: 87 us -> none
    add x16 -> x0, other arithmetic: 79.7 us -> none  [accumulate(): total + weight_row[:, None, None, None, None, None] * powers[None]]
    reduce_scatter x1 -> x0, waiting for transfers between devices: 59.4 us -> none  [local(): lax.psum_scatter(partial_sums, 'snap', scatter_dimension=5, tiled=True)]
    squeeze x34 -> x0, local copies, waits for them, and re-layouts: 39.5 us -> none  [the longest x32 35 us: weighted_powers(): sums, _ = lax.scan(accumulate, start, (weights, comp_u, comp_v, comp_w))]
    another operation x35 -> x0, other arithmetic: 34.4 us -> none  [the longest x32 34.2 us: accumulate(): jnp.stack([omega, squared, squared * omega, squared * squared], axis=1)]
    ppermute x2 -> x0, waiting for transfers between devices: 30.9 us -> none  [the longest x1 30.9 us: extended(): before = lax.ppermute(last, axis, up)]
    sub x32 -> x0, other arithmetic: 26 us -> none  [the longest x16 16.7 us: vorticity_of(): omega_x = central(comp_w, 1) - central(comp_v, 2)]
  transfers between devices with their start and end apart: 3 -> 0, of which waited for: 2 -> 0; matrix products, arithmetic and copies ran while one was open for 3% -> 0% of each run, Pallas kernels for 0% -> 0%
where the time goes in v1:
time: 110 us
  Pallas kernels  107 us (97%)
  local copies, waits for them, and re-layouts  3.32 us (3%)
    pallas_call x1, Pallas kernels, local(): pl.pallas_call(kernel, out_shape=jax.ShapeDtypeStruct((3, 3, 4, NP, NY, L...  107 us
    unnamed x1, local copies, waits for them, and re-layouts  3.32 us

profile of v1, /device:TPU:1, one launch (start us, length us, event | category | flops | bytes accessed | tf_op | source)
XLA Modules:
  0.0 110.0 jit_solution(17369405165525634449)
XLA Ops:
  0.0 106.7 %shard_map.64 = f32[3,3,4,8,16,128]{5,4,3,2,1,0:T(8,128)} custom-call(bf16[16,3,8,16,512]{4,3,2,1,0:T(8,128)(2,1)} %vel_hbm.1, s32[16]{0:T(128)} %bins.1, bf16[2,128,128]{2,1,0:T(8,128)(2,1)} %constant.8.clone.left_w, bf16[2,64,256]{2,1,0:T(8,128)(2,1)} %constant.9.clone.left_vu, bf16[64,64]{1,0:T(8,128)(2,1)} %constant.10.clone.left_halo, ...), custom_call_target="tpu_custom_call" | custom-call | tf_op jit(solution)/shard_map/pallas_call | solution.py:270
  106.7 3.3 %copy.8 = f32[3,3,4,8,16,128]{5,4,3,2,1,0:T(8,128)} copy(f32[3,3,4,8,16,128]{5,4,3,2,1,0:T(8,128)} %shard_map.64) | data formatting | bytes 4718592

commit v2 on v1

--- a/solution.py
+++ b/solution.py
@@ -15,6 +15,7 @@
 PLANES = ((2, 3, 4, 5), (0, 1, 6, 7))
 NS, NP, NY, NZ = 16, 8, 16, 512
 LANES = 128
+TOP = 32766.0
 
 
 def band(n):
@@ -52,10 +53,11 @@
 
 
 def kernel(
-    vel_hbm, bins, left_w, left_vu, left_halo, right_z, out,
-    vel, halo, omega, weights, sums, mate, cross_out, cross_in, gram_out, gram_in,
-    load_sem, halo_send, halo_recv, mate_send, mate_recv, cross_send, cross_recv, gram_send, gram_recv,
-):
+    vel_hbm, bins, *refs):
+    consts_hbm, out, consts, refs = refs[:4], refs[4], refs[5:9], refs[9:]
+    left_w, left_vu, left_halo, right_z = consts
+    (vel, halo, omega, weights, sums, mate, cross_out, cross_in, step_out, step_in, gram_out, gram_in,
+    load_sem, halo_send, halo_recv, mate_send, mate_recv, cross_send, cross_recv, step_send, step_recv, gram_send, gram_recv, const_sem) = refs
     snap, slab = lax.axis_index("snap"), lax.axis_index("slab")
     slabs = lax.axis_size("slab")
     core, chip = snap % 2, snap // 2
@@ -72,6 +74,11 @@
 
     load = pltpu.make_async_copy(vel_hbm, vel, load_sem)
     load.start()
+    const_loads = [
+        pltpu.make_async_copy(consts_hbm[n], consts[n], const_sem.at[n]) for n in range(4)
+    ]
+    for const_load in const_loads:
+        const_load.start()
 
     barrier = pltpu.get_barrier_semaphore()
     for peer in snap_peers:
@@ -127,6 +134,8 @@
         )
 
     load.wait()
+    for const_load in const_loads:
+        const_load.wait()
 
     def derive(i, p):
         z = zone(i)
@@ -195,6 +204,13 @@
             device_id=cross_peer, device_id_type=MESH,
         )
 
+    def step_copy(p):
+        return pltpu.make_async_remote_copy(
+            src_ref=step_out.at[p], dst_ref=step_in.at[p],
+            send_sem=step_send.at[p], recv_sem=step_recv.at[p],
+            device_id=cross_peer, device_id_type=MESH,
+        )
+
     for p in range(2):
         for i in range(4):
             if p == 1:
@@ -214,10 +230,15 @@
 
                 def add(t, carry, p=p):
                     for j in range(3):
-                        cross_out[p, j, t] = sums[1, p, j, t] + mate[0, p, j, t]
+                        total = sums[1, p, j, t] + mate[0, p, j, t]
+                        top = jnp.maximum(jnp.max(jnp.abs(total), axis=(0, 1))[None], 1e-33)
+                        code = jnp.round(total * (TOP / top)[None]).astype(jnp.int32)
+                        cross_out[p, j, t] = code.astype(jnp.int16).reshape(4, NY, LANES)
+                        step_out[p, j, pl.ds(t, 1)] = top * (1.0 / TOP)
                     return carry
 
                 lax.fori_loop(0, 12, add, 0)
+                step_copy(p).start()
                 cross_copy(p).start()
 
     for d in range(3):
@@ -236,10 +257,17 @@
 
     for p in range(2):
         mate_copy(1, p).wait_recv()
+        step_copy(p).wait_recv()
         cross_copy(p).wait_recv()
 
         def solve(t, carry, p=p):
-            total = [sums[3, p, j, t] + mate[1, p, j, t] + cross_in[p, j, t] for j in range(3)]
+            total = [
+                sums[3, p, j, t]
+                + mate[1, p, j, t]
+                + cross_in[p, j, t].astype(jnp.int32).astype(jnp.float32).reshape(8, 8, LANES)
+                * step_in[p, j, pl.ds(t, 1)][None]
+                for j in range(3)
+            ]
             for n in range(3):
                 fit = sum(inverse[n][j][None] * total[j] for j in range(3)).reshape(4, NY, LANES)
                 if p == 0:
@@ -258,32 +286,36 @@
                 halo_copy(i, side).wait_send()
     for p in range(2):
         cross_copy(p).wait_send()
+        step_copy(p).wait_send()
         for half in range(2):
             mate_copy(half, p).wait_send()
 
 
 def local(velocity, phase_bins):
     consts = [jnp.asarray(m, jnp.bfloat16) for m in stencils()]
-    vmem = pl.BlockSpec(memory_space=pltpu.VMEM)
+    hbm = pl.BlockSpec(memory_space=pl.ANY)
     f32, bf16, dma = jnp.float32, jnp.bfloat16, pltpu.SemaphoreType.DMA
     block = (3, 12, 8, 8, LANES)
     return pl.pallas_call(
         kernel,
         out_shape=jax.ShapeDtypeStruct((3, 3, 4, NP, NY, LANES), f32),
-        in_specs=[pl.BlockSpec(memory_space=pl.ANY), pl.BlockSpec(memory_space=pltpu.SMEM)] + [vmem] * 4,
-        out_specs=vmem,
-        scratch_shapes=[
+        in_specs=[hbm, pl.BlockSpec(memory_space=pltpu.SMEM)] + [hbm] * 4,
+        out_specs=pl.BlockSpec(memory_space=pltpu.VMEM),
+        scratch_shapes=[pltpu.VMEM(c.shape, bf16) for c in consts]
+        + [
             pltpu.VMEM((NS, 3, NP, NY, NZ), bf16),
             pltpu.VMEM((4, NS, 2, 2, 2, NY, LANES), bf16),
             pltpu.VMEM((NS, 3, 8, 8, LANES), f32),
             pltpu.VMEM((2, NS, 8, LANES), f32),
             pltpu.VMEM((4, 2) + block, f32),
             pltpu.VMEM((2, 2) + block, f32),
-            pltpu.VMEM((2,) + block, f32),
-            pltpu.VMEM((2,) + block, f32),
+            pltpu.VMEM((2, 3, 12, 4, NY, LANES), jnp.int16),
+            pltpu.VMEM((2, 3, 12, 4, NY, LANES), jnp.int16),
+            pltpu.VMEM((2, 3, 16, LANES), f32),
+            pltpu.VMEM((2, 3, 16, LANES), f32),
             pltpu.VMEM((5, 8, LANES), f32),
             pltpu.VMEM((3, 5, 8, LANES), f32),
-            dma, dma((4, 2)), dma((4, 2)), dma((2, 2)), dma((2, 2)), dma((2,)), dma((2,)), dma((3,)), dma((3,)),
+            dma, dma((4, 2)), dma((4, 2)), dma((2, 2)), dma((2, 2)), dma((2,)), dma((2,)), dma((2,)), dma((2,)), dma((3,)), dma((3,)), dma((4,)),
         ],
         compiler_params=pltpu.CompilerParams(collective_id=0, has_side_effects=True),
     )(velocity, phase_bins, *consts)

time: 110 us -> 85.6 us (0.78)
  Pallas kernels: 107 us -> 82.2 us
    pallas_call x1, Pallas kernels: 107 us -> 82.2 us  [local(): pl.pallas_call(kernel, out_shape=jax.ShapeDtypeStruct((3, 3, 4, NP, NY, L...]
where the time goes in v2:
time: 85.6 us; the launch traced here: 85.5 us
  Pallas kernels  82.2 us (96%)
  local copies, waits for them, and re-layouts  3.32 us (4%)
    pallas_call x1, Pallas kernels, local(): pl.pallas_call(kernel, out_shape=jax.ShapeDtypeStruct((3, 3, 4, NP, NY, L...  82.2 us
    unnamed x1, local copies, waits for them, and re-layouts  3.32 us

profile of v2, /device:TPU:1, one launch (start us, length us, event | category | flops | bytes accessed | tf_op | source)
XLA Modules:
  0.0 85.5 jit_solution(4281508866568489746)
XLA Ops:
  0.0 82.2 %shard_map.64 = f32[3,3,4,8,16,128]{5,4,3,2,1,0:T(8,128)} custom-call(bf16[16,3,8,16,512]{4,3,2,1,0:T(8,128)(2,1)} %vel_hbm.1, s32[16]{0:T(128)} %bins.1, bf16[2,128,128]{2,1,0:T(8,128)(2,1)} %constant.8.clone.refs_0_, bf16[2,64,256]{2,1,0:T(8,128)(2,1)} %constant.9.clone.refs_1_, bf16[64,64]{1,0:T(8,128)(2,1)} %constant.10.clone.refs_2_, ...), custom_call_target="tpu_custom_call" | custom-call | tf_op jit(solution)/shard_map/pallas_call | solution.py:299
  82.2 3.3 %copy.8 = f32[3,3,4,8,16,128]{5,4,3,2,1,0:T(8,128)} copy(f32[3,3,4,8,16,128]{5,4,3,2,1,0:T(8,128)} %shard_map.64) | data formatting | bytes 4718592

commit v3 on v2

--- a/solution.py
+++ b/solution.py
@@ -18,34 +18,33 @@
 TOP = 32766.0
 
 
-def band(n):
-    d = np.zeros((n, n), np.float32)
-    for i in range(n):
-        for o, c in ((1, NEAR), (-1, -NEAR), (2, -WIDE), (-2, WIDE)):
-            if 0 <= i + o < n:
-                d[i, i + o] = c
-    return d
-
-
-def stencils():
-    along_y = np.kron(np.eye(NP, dtype=np.float32), band(NY))
-    along_x = np.kron(band(NP + 4), np.eye(NY, dtype=np.float32))
-    left_w, left_vu, left_halo = [], [], []
-    for planes in PLANES:
-        rows = np.concatenate([np.arange(p * NY, (p + 1) * NY) for p in planes])
-        dy = along_y[rows]
-        dx_ext = along_x[rows + 2 * NY]
-        dx = dx_ext[:, 2 * NY : 2 * NY + NP * NY]
-        halo = np.concatenate([dx_ext[:, : 2 * NY], dx_ext[:, -2 * NY :]], axis=1)
-        left_w.append(np.concatenate([dy, -dx], axis=0))
-        left_vu.append(np.concatenate([dx, -dy], axis=1))
-        left_halo.append(halo)
-    return [
-        np.stack(left_w),
-        np.stack(left_vu),
-        left_halo[1],
-        band(NZ).T.copy(),
-    ]
+def band(d):
+    near = jnp.where(d == 1, NEAR, jnp.where(d == -1, -NEAR, 0.0))
+    return near + jnp.where(d == 2, -WIDE, jnp.where(d == -2, WIDE, 0.0))
+
+
+def grid(rows, cols):
+    return [lax.broadcasted_iota(jnp.int32, (rows, cols), n) for n in (0, 1)]
+
+
+def fill_stencils(left_w, left_vu, left_halo, right_z):
+    bf16 = jnp.bfloat16
+    for p in range(2):
+        r, c = grid(64, NP * NY)
+        plane = (r >> 4) + (2 if p == 0 else (r >> 5) * 4)
+        same_y, same_x = (r & 15) == (c & 15), plane == (c >> 4)
+        dx = jnp.where(same_y, band((c >> 4) - plane), 0.0)
+        dy = jnp.where(same_x, band((c & 15) - (r & 15)), 0.0)
+        left_w[p, 0:64] = dy.astype(bf16)
+        left_w[p, 64:128] = (-dx).astype(bf16)
+        left_vu[p, :, 0:128] = dx.astype(bf16)
+        left_vu[p, :, 128:256] = (-dy).astype(bf16)
+    r, c = grid(64, 64)
+    plane = (r >> 4) + (r >> 5) * 4
+    beyond = (c >> 4) - 2 + (c >> 5) * 8
+    left_halo[...] = jnp.where((r & 15) == (c & 15), band(beyond - plane), 0.0).astype(bf16)
+    r, c = grid(NZ, NZ)
+    right_z[...] = band(r - c).astype(bf16)
 
 
 def dot(a, b):
@@ -53,10 +52,10 @@
 
 
 def kernel(
-    vel_hbm, bins, *refs):
-    consts_hbm, out, consts, refs = refs[:4], refs[4], refs[5:9], refs[9:]
+    vel_hbm, bins_hbm, out, *refs):
+    consts, refs = refs[:4], refs[4:]
     left_w, left_vu, left_halo, right_z = consts
-    (vel, halo, omega, weights, sums, mate, cross_out, cross_in, step_out, step_in, gram_out, gram_in,
+    (bins, vel, halo, omega, weights, sums, mate, cross_out, cross_in, steps, step_out, step_in, gram_out, gram_in,
     load_sem, halo_send, halo_recv, mate_send, mate_recv, cross_send, cross_recv, step_send, step_recv, gram_send, gram_recv, const_sem) = refs
     snap, slab = lax.axis_index("snap"), lax.axis_index("slab")
     slabs = lax.axis_size("slab")
@@ -74,11 +73,8 @@
 
     load = pltpu.make_async_copy(vel_hbm, vel, load_sem)
     load.start()
-    const_loads = [
-        pltpu.make_async_copy(consts_hbm[n], consts[n], const_sem.at[n]) for n in range(4)
-    ]
-    for const_load in const_loads:
-        const_load.start()
+    bins_load = pltpu.make_async_copy(bins_hbm, bins, const_sem)
+    bins_load.start()
 
     barrier = pltpu.get_barrier_semaphore()
     for peer in snap_peers:
@@ -112,6 +108,8 @@
             for i in range(4):
                 halo[i, :, :, side] = jnp.zeros((NS, 2, 2, NY, LANES), jnp.bfloat16)
 
+    fill_stencils(*consts)
+    bins_load.wait()
     zero = jnp.zeros((8, LANES), jnp.float32)
 
     def weigh(s, g):
@@ -123,6 +121,7 @@
         weights[1, s] = n
         return (g[0] + c, g[1] + n, g[2] + c * c, g[3] + c * n, g[4] + n * n)
 
+    steps[...] = jnp.zeros((3, 16, LANES), jnp.float32)
     for n, value in enumerate(lax.fori_loop(0, NS, weigh, (zero,) * 5)):
         gram_out[n] = value
 
@@ -134,8 +133,6 @@
         )
 
     load.wait()
-    for const_load in const_loads:
-        const_load.wait()
 
     def derive(i, p):
         z = zone(i)
@@ -231,13 +228,15 @@
                 def add(t, carry, p=p):
                     for j in range(3):
                         total = sums[1, p, j, t] + mate[0, p, j, t]
-                        top = jnp.maximum(jnp.max(jnp.abs(total), axis=(0, 1))[None], 1e-33)
-                        code = jnp.round(total * (TOP / top)[None]).astype(jnp.int32)
+                        top = jnp.maximum(jnp.max(jnp.abs(total), axis=(0, 1))[None], 1e-32)
+                        step = (top * ((1.0 + 2.0**-7) / TOP)).astype(jnp.bfloat16).astype(jnp.float32)
+                        code = jnp.round(total * (1.0 / step)[None]).astype(jnp.int32)
                         cross_out[p, j, t] = code.astype(jnp.int16).reshape(4, NY, LANES)
-                        step_out[p, j, pl.ds(t, 1)] = top * (1.0 / TOP)
+                        steps[j, pl.ds(t, 1)] = step
                     return carry
 
                 lax.fori_loop(0, 12, add, 0)
+                step_out[p] = steps[...].astype(jnp.bfloat16)
                 step_copy(p).start()
                 cross_copy(p).start()
 
@@ -258,6 +257,7 @@
     for p in range(2):
         mate_copy(1, p).wait_recv()
         step_copy(p).wait_recv()
+        steps[...] = step_in[p].astype(jnp.float32)
         cross_copy(p).wait_recv()
 
         def solve(t, carry, p=p):
@@ -265,7 +265,7 @@
                 sums[3, p, j, t]
                 + mate[1, p, j, t]
                 + cross_in[p, j, t].astype(jnp.int32).astype(jnp.float32).reshape(8, 8, LANES)
-                * step_in[p, j, pl.ds(t, 1)][None]
+                * steps[j, pl.ds(t, 1)][None]
                 for j in range(3)
             ]
             for n in range(3):
@@ -292,17 +292,17 @@
 
 
 def local(velocity, phase_bins):
-    consts = [jnp.asarray(m, jnp.bfloat16) for m in stencils()]
-    hbm = pl.BlockSpec(memory_space=pl.ANY)
+    hbm = pl.BlockSpec(memory_space=pltpu.HBM)
     f32, bf16, dma = jnp.float32, jnp.bfloat16, pltpu.SemaphoreType.DMA
     block = (3, 12, 8, 8, LANES)
     return pl.pallas_call(
         kernel,
-        out_shape=jax.ShapeDtypeStruct((3, 3, 4, NP, NY, LANES), f32),
-        in_specs=[hbm, pl.BlockSpec(memory_space=pltpu.SMEM)] + [hbm] * 4,
+        out_shape=pltpu.VMEM((3, 3, 4, NP, NY, LANES), f32),
+        in_specs=[hbm] * 2,
         out_specs=pl.BlockSpec(memory_space=pltpu.VMEM),
-        scratch_shapes=[pltpu.VMEM(c.shape, bf16) for c in consts]
+        scratch_shapes=[pltpu.VMEM(c, bf16) for c in ((2, 128, 128), (2, 64, 256), (64, 64), (NZ, NZ))]
         + [
+            pltpu.SMEM((NS,), jnp.int32),
             pltpu.VMEM((NS, 3, NP, NY, NZ), bf16),
             pltpu.VMEM((4, NS, 2, 2, 2, NY, LANES), bf16),
             pltpu.VMEM((NS, 3, 8, 8, LANES), f32),
@@ -311,14 +311,15 @@
             pltpu.VMEM((2, 2) + block, f32),
             pltpu.VMEM((2, 3, 12, 4, NY, LANES), jnp.int16),
             pltpu.VMEM((2, 3, 12, 4, NY, LANES), jnp.int16),
-            pltpu.VMEM((2, 3, 16, LANES), f32),
-            pltpu.VMEM((2, 3, 16, LANES), f32),
+            pltpu.VMEM((3, 16, LANES), f32),
+            pltpu.VMEM((2, 3, 16, LANES), bf16),
+            pltpu.VMEM((2, 3, 16, LANES), bf16),
             pltpu.VMEM((5, 8, LANES), f32),
             pltpu.VMEM((3, 5, 8, LANES), f32),
-            dma, dma((4, 2)), dma((4, 2)), dma((2, 2)), dma((2, 2)), dma((2,)), dma((2,)), dma((2,)), dma((2,)), dma((3,)), dma((3,)), dma((4,)),
+            dma, dma((4, 2)), dma((4, 2)), dma((2, 2)), dma((2, 2)), dma((2,)), dma((2,)), dma((2,)), dma((2,)), dma((3,)), dma((3,)), dma,
         ],
         compiler_params=pltpu.CompilerParams(collective_id=0, has_side_effects=True),
-    )(velocity, phase_bins, *consts)
+    )(velocity, phase_bins)
 
 
 def solution(mesh):

time: 85.6 us -> 81 us (0.946)
  Pallas kernels: 82.2 us -> 79.5 us
  local copies, waits for them, and re-layouts: 3.32 us -> 1.41 us
    pallas_call x1, Pallas kernels: 82.2 us -> 79.5 us  [local(): pl.pallas_call(kernel, out_shape=pltpu.VMEM((3, 3, 4, NP, NY, LANES), f32...]
    unnamed x1, local copies, waits for them, and re-layouts: 3.32 us -> 1.41 us
where the time goes in v3:
time: 81 us; the launch traced here: 80.9 us
  Pallas kernels  79.5 us (98%)
  local copies, waits for them, and re-layouts  1.41 us (2%)
    pallas_call x1, Pallas kernels, local(): pl.pallas_call(kernel, out_shape=pltpu.VMEM((3, 3, 4, NP, NY, LANES), f32...  79.5 us

profile of v3, /device:TPU:1, one launch (start us, length us, event | category | flops | bytes accessed | tf_op | source)
XLA Modules:
  0.0 80.9 jit_solution(11578740651857268445)
XLA Ops:
  0.0 79.5 %shard_map.28 = f32[3,3,4,8,16,128]{5,4,3,2,1,0:T(8,128)S(1)} custom-call(bf16[16,3,8,16,512]{4,3,2,1,0:T(8,128)(2,1)} %vel_hbm.1, s32[16]{0:T(128)} %bins_hbm.1), custom_call_target="tpu_custom_call" | custom-call | tf_op jit(solution)/shard_map/pallas_call | solution.py:298
  79.5 1.4 %copy.4 = f32[3,3,4,8,16,128]{5,4,3,2,1,0:T(8,128)} copy(f32[3,3,4,8,16,128]{5,4,3,2,1,0:T(8,128)S(1)} %shard_map.28) | data formatting | bytes 4718592

commit v4 on v3

--- a/solution.py
+++ b/solution.py
@@ -194,10 +194,11 @@
             device_id=mate_peer, device_id_type=MESH,
         )
 
-    def cross_copy(p):
-        return pltpu.make_async_remote_copy(
-            src_ref=cross_out.at[p], dst_ref=cross_in.at[p],
-            send_sem=cross_send.at[p], recv_sem=cross_recv.at[p],
+    def cross_copy(p, c):
+        part = pl.ds(4 * c, 4)
+        return pltpu.make_async_remote_copy(
+            src_ref=cross_out.at[p, :, part], dst_ref=cross_in.at[p, :, part],
+            send_sem=cross_send.at[p, c], recv_sem=cross_recv.at[p, c],
             device_id=cross_peer, device_id_type=MESH,
         )
 
@@ -238,7 +239,8 @@
                 lax.fori_loop(0, 12, add, 0)
                 step_out[p] = steps[...].astype(jnp.bfloat16)
                 step_copy(p).start()
-                cross_copy(p).start()
+                for c in range(3):
+                    cross_copy(p, c).start()
 
     for d in range(3):
         gram_copy(d).wait()
@@ -256,14 +258,20 @@
 
     for p in range(2):
         mate_copy(1, p).wait_recv()
+
+        def fold(t, carry, p=p):
+            for j in range(3):
+                sums[3, p, j, t] = sums[3, p, j, t] + mate[1, p, j, t]
+            return carry
+
+        lax.fori_loop(0, 12, fold, 0)
+    for p in range(2):
         step_copy(p).wait_recv()
         steps[...] = step_in[p].astype(jnp.float32)
-        cross_copy(p).wait_recv()
 
         def solve(t, carry, p=p):
             total = [
                 sums[3, p, j, t]
-                + mate[1, p, j, t]
                 + cross_in[p, j, t].astype(jnp.int32).astype(jnp.float32).reshape(8, 8, LANES)
                 * steps[j, pl.ds(t, 1)][None]
                 for j in range(3)
@@ -277,7 +285,9 @@
                     out[n, t // 4, t % 4, 6:8] = fit[2:]
             return carry
 
-        lax.fori_loop(0, 12, solve, 0)
+        for c in range(3):
+            cross_copy(p, c).wait_recv()
+            lax.fori_loop(4 * c, 4 * c + 4, solve, 0)
 
     for i in range(4):
         for side, cond in ((0, has_hi), (1, has_lo)):
@@ -285,7 +295,8 @@
             def _(i=i, side=side):
                 halo_copy(i, side).wait_send()
     for p in range(2):
-        cross_copy(p).wait_send()
+        for c in range(3):
+            cross_copy(p, c).wait_send()
         step_copy(p).wait_send()
         for half in range(2):
             mate_copy(half, p).wait_send()
@@ -316,7 +327,7 @@
             pltpu.VMEM((2, 3, 16, LANES), bf16),
             pltpu.VMEM((5, 8, LANES), f32),
             pltpu.VMEM((3, 5, 8, LANES), f32),
-            dma, dma((4, 2)), dma((4, 2)), dma((2, 2)), dma((2, 2)), dma((2,)), dma((2,)), dma((2,)), dma((2,)), dma((3,)), dma((3,)), dma,
+            dma, dma((4, 2)), dma((4, 2)), dma((2, 2)), dma((2, 2)), dma((2, 3)), dma((2, 3)), dma((2,)), dma((2,)), dma((3,)), dma((3,)), dma,
         ],
         compiler_params=pltpu.CompilerParams(collective_id=0, has_side_effects=True),
     )(velocity, phase_bins)

time: 81 us -> 80.8 us (level)
  no operation moved by 1% of the time
where the time goes in v4:
time: 80.8 us; the launch traced here: 80.7 us
  Pallas kernels  79.3 us (98%)
  local copies, waits for them, and re-layouts  1.41 us (2%)
    pallas_call x1, Pallas kernels, local(): pl.pallas_call(kernel, out_shape=pltpu.VMEM((3, 3, 4, NP, NY, LANES), f32...  79.3 us

profile of v4, /device:TPU:1, one launch (start us, length us, event | category | flops | bytes accessed | tf_op | source)
XLA Modules:
  0.0 80.7 jit_solution(14573393996765966762)
XLA Ops:
  0.0 79.3 %shard_map.28 = f32[3,3,4,8,16,128]{5,4,3,2,1,0:T(8,128)S(1)} custom-call(bf16[16,3,8,16,512]{4,3,2,1,0:T(8,128)(2,1)} %vel_hbm.1, s32[16]{0:T(128)} %bins_hbm.1), custom_call_target="tpu_custom_call" | custom-call | tf_op jit(solution)/shard_map/pallas_call | solution.py:309
  79.3 1.4 %copy.4 = f32[3,3,4,8,16,128]{5,4,3,2,1,0:T(8,128)} copy(f32[3,3,4,8,16,128]{5,4,3,2,1,0:T(8,128)S(1)} %shard_map.28) | data formatting | bytes 4718592

commit v5 on v3

--- a/solution.py
+++ b/solution.py
@@ -291,11 +291,21 @@
             mate_copy(half, p).wait_send()
 
 
+def put(fit, out, sem):
+    copies = [
+        pltpu.make_async_copy(fit.at[n, m], out.at[n, m], sem.at[n, m]) for n in range(3) for m in range(3)
+    ]
+    for copy in copies:
+        copy.start()
+    for copy in copies:
+        copy.wait()
+
+
 def local(velocity, phase_bins):
     hbm = pl.BlockSpec(memory_space=pltpu.HBM)
     f32, bf16, dma = jnp.float32, jnp.bfloat16, pltpu.SemaphoreType.DMA
     block = (3, 12, 8, 8, LANES)
-    return pl.pallas_call(
+    fit = pl.pallas_call(
         kernel,
         out_shape=pltpu.VMEM((3, 3, 4, NP, NY, LANES), f32),
         in_specs=[hbm] * 2,
@@ -320,6 +330,14 @@
         ],
         compiler_params=pltpu.CompilerParams(collective_id=0, has_side_effects=True),
     )(velocity, phase_bins)
+    return pl.pallas_call(
+        put,
+        out_shape=jax.ShapeDtypeStruct(fit.shape, f32),
+        in_specs=[pl.BlockSpec(memory_space=pltpu.VMEM)],
+        out_specs=hbm,
+        scratch_shapes=[dma((3, 3))],
+        compiler_params=pltpu.CompilerParams(vmem_limit_bytes=8 * 1024 * 1024),
+    )(fit)
 
 
 def solution(mesh):

time: 81 us -> 81.1 us (level)
  Pallas kernels: 79.5 us -> 81 us
  local copies, waits for them, and re-layouts: 1.41 us -> 0 us
    pallas_call x0 -> x1, Pallas kernels: none -> 1.47 us  [local(): pl.pallas_call(put, out_shape=jax.ShapeDtypeStruct(fit.shape, f32), in_sp...]
    unnamed x1 -> x0, local copies, waits for them, and re-layouts: 1.41 us -> none
where the time goes in v5:
time: 81.1 us; the launch traced here: 81 us
  Pallas kernels  81 us (100%)
    pallas_call x1, Pallas kernels, local(): pl.pallas_call(kernel, out_shape=pltpu.VMEM((3, 3, 4, NP, NY, LANES), f32...  79.5 us

profile of v5, /device:TPU:1, one launch (start us, length us, event | category | flops | bytes accessed | tf_op | source)
XLA Modules:
  0.0 81.0 jit_solution(9742817411102479575)
XLA Ops:
  0.0 79.5 %shard_map.28.fit = f32[3,3,4,8,16,128]{5,4,3,2,1,0:T(8,128)S(1)} custom-call(bf16[16,3,8,16,512]{4,3,2,1,0:T(8,128)(2,1)} %vel_hbm.1, s32[16]{0:T(128)} %bins_hbm.1), custom_call_target="tpu_custom_call" | custom-call | tf_op jit(solution)/shard_map/pallas_call | solution.py:308
  79.5 1.5 %shard_map.29 = f32[3,3,4,8,16,128]{5,4,3,2,1,0:T(8,128)} custom-call(f32[3,3,4,8,16,128]{5,4,3,2,1,0:T(8,128)S(1)} %shard_map.28.fit), custom_call_target="tpu_custom_call" | custom-call | tf_op jit(solution)/shard_map/pallas_call | solution.py:333

commit v6 on v3

--- a/solution.py
+++ b/solution.py
@@ -72,7 +72,6 @@
         return pl.ds(pl.multiple_of((side * 2 + (core + 1 + i) % 2) * LANES, LANES), LANES)
 
     load = pltpu.make_async_copy(vel_hbm, vel, load_sem)
-    load.start()
     bins_load = pltpu.make_async_copy(bins_hbm, bins, const_sem)
     bins_load.start()
 
@@ -101,6 +100,7 @@
             @pl.when(cond)
             def _(i=i, side=side):
                 halo_copy(i, side).start()
+    load.start()
 
     for side, cond in ((0, has_lo), (1, has_hi)):
         @pl.when(jnp.logical_not(cond))

time: 81 us -> 81 us (level)
  no operation moved by 1% of the time
where the time goes in v6:
time: 81 us; the launch traced here: 80.9 us
  Pallas kernels  79.5 us (98%)
  local copies, waits for them, and re-layouts  1.41 us (2%)
    pallas_call x1, Pallas kernels, local(): pl.pallas_call(kernel, out_shape=pltpu.VMEM((3, 3, 4, NP, NY, LANES), f32...  79.5 us

profile of v6, /device:TPU:1, one launch (start us, length us, event | category | flops | bytes accessed | tf_op | source)
XLA Modules:
  0.0 80.9 jit_solution(6303839366135480860)
XLA Ops:
  0.0 79.5 %shard_map.28 = f32[3,3,4,8,16,128]{5,4,3,2,1,0:T(8,128)S(1)} custom-call(bf16[16,3,8,16,512]{4,3,2,1,0:T(8,128)(2,1)} %vel_hbm.1, s32[16]{0:T(128)} %bins_hbm.1), custom_call_target="tpu_custom_call" | custom-call | tf_op jit(solution)/shard_map/pallas_call | solution.py:298
  79.5 1.4 %copy.4 = f32[3,3,4,8,16,128]{5,4,3,2,1,0:T(8,128)} copy(f32[3,3,4,8,16,128]{5,4,3,2,1,0:T(8,128)S(1)} %shard_map.28) | data formatting | bytes 4718592
